TPU v7x, 128 devices: a whole 4x4x4 slice. The times are simulated.
128 devices in a mesh: section: 2 (over core), dp: 4 (over x), mp: 16 (over z, y).
Axes of the slice: x: 4, y: 4, z: 4, core: 2. Of those that a mesh axis runs over, the one named last changes fastest.
Arguments:
- segment_input: bfloat16 [2, 4, 256, 2048], P(None, 'dp', None, 'mp'), may hold values from -6 to 6
- out_grad: bfloat16 [2, 4, 256, 2048], P(None, 'dp', None, 'mp'), may hold values from -6 to 6
- pool_tokens: bfloat16 [16, 4, 128, 896], P('section', 'dp'), may hold values from -6 to 6
- neighbour_ids: int32 [2, 4, 4, 4], P(None, 'dp'), may hold values from 0 to 15, as said below
- neighbour_counts: int32 [2, 4, 4], P(None, 'dp'), may hold values from 1 to 4
- enc_gain: float32 [896], replicated, may hold values from 0.5 to 1.5
- enc_up: bfloat16 [896, 4096], P(None, 'mp'), may hold values from -0.1875 to 0.1875
- enc_down: bfloat16 [4096, 896], P(None, 'mp'), may hold values from -0.09375 to 0.09375
- norm_gain: float32 [2, 2048], P('section'), may hold values from 0.5 to 1.5
- w_query: bfloat16 [2, 2048, 4096], P('section', None, 'mp'), may hold values from -0.125 to 0.125
- w_key: bfloat16 [2, 896, 4096], P('section', None, 'mp'), may hold values from -0.1875 to 0.1875
- w_value: bfloat16 [2, 896, 4096], P('section', None, 'mp'), may hold values from -0.1875 to 0.1875
- w_out: bfloat16 [2, 4096, 2048], P('section', None, 'mp'), may hold values from -0.09375 to 0.09375
Outputs:
- grad_key: bfloat16 [2, 896, 4096], P('section', None, 'mp')
- grad_value: bfloat16 [2, 896, 4096], P('section', None, 'mp')
Inputs may be any that keep to these rules, and one draw needn't show every extreme that they name: `neighbour_ids`: the 4 slots of one stretch name distinct pool stretches.
All inputs are finite; a program needn't handle non-finite values.
Results may differ from a plain program's by a relative error of at most 0.025.
Values may be sent and summed in bfloat16 or wider, within the bound.
A program may use at most 128 MiB of HBM per device.

v0:
```python
import jax
import jax.numpy as jnp
from jax import lax
from jax.sharding import PartitionSpec as P

HEAD = 128
NT = 128
EPSILON = 1e-05


def passed_along(value, axis, by):
    peers = lax.axis_size(axis)
    pairs = [(i, i + by) for i in range(peers) if 0 <= i + by < peers]
    return lax.ppermute(value, axis, pairs)


def rms_scale(values):
    return lax.rsqrt(jnp.mean(values * values, axis=-1, keepdims=True) + EPSILON)


def collect(tensor):
    return lax.all_gather(tensor, "mp", axis=1, tiled=True)


def collect_pair(first, second):
    return (
        lax.all_gather(first, "mp", axis=1, tiled=True),
        lax.all_gather(second, "mp", axis=1, tiled=True),
    )


def pass_on(tensor, offset):
    return passed_along(tensor, "section", offset)


def attend(queries, key_block, value_block, usable):
    scores = jnp.einsum("cqhe,ckhe->chqk", queries, key_block, preferred_element_type=jnp.float32)
    scores = jnp.where(usable[:, None, None, :], scores, -1e30)
    weights = jax.nn.softmax(scores, axis=-1)
    weights_bf = weights.astype(jnp.bfloat16)
    attended = jnp.einsum(
        "chqk,ckhe->cqhe", weights_bf, value_block, preferred_element_type=jnp.float32
    )
    return (weights, weights_bf, attended.astype(jnp.bfloat16))


def attend_back(queries, key_block, value_block, weights, weights_bf, grad_attended):
    grad_weights = jnp.einsum(
        "cqhe,ckhe->chqk", grad_attended, value_block, preferred_element_type=jnp.float32
    )
    grad_scores = weights * (grad_weights - jnp.sum(weights * grad_weights, axis=-1, keepdims=True))
    grad_values = jnp.einsum(
        "chqk,cqhe->ckhe", weights_bf, grad_attended, preferred_element_type=jnp.float32
    ).astype(jnp.bfloat16)
    grad_keys = jnp.einsum("chqk,cqhe->ckhe", grad_scores, queries.astype(jnp.float32)).astype(
        jnp.bfloat16
    )
    grad_queries = jnp.einsum("chqk,ckhe->cqhe", grad_scores, key_block.astype(jnp.float32))
    return (grad_keys, grad_values, grad_queries)


def front(rows_in, gain_full, query_cols, key_block, value_block, usable, head_count):
    rows_wide = rows_in.astype(jnp.float32)
    inv_rms = rms_scale(rows_wide)
    normed = (rows_wide * inv_rms * gain_full).astype(jnp.bfloat16)
    query_raw = jnp.dot(normed, query_cols, preferred_element_type=jnp.float32)
    queries = (query_raw * HEAD ** (-0.5)).astype(jnp.bfloat16)
    queries = queries.reshape(key_block.shape[0], -1, head_count, HEAD)
    weights, weights_bf, attended = attend(queries, key_block, value_block, usable)
    return (inv_rms, query_raw, queries, weights, weights_bf, attended)


def on_device(
    segment_input,
    out_grad,
    pool_tokens,
    neighbour_ids,
    neighbour_counts,
    enc_gain,
    enc_up,
    enc_down,
    norm_gain,
    w_query,
    w_key,
    w_value,
    w_out,
):
    model_count = lax.axis_size("mp")
    model_index = lax.axis_index("mp")
    segment_count = lax.axis_size("section")
    segment_index = lax.axis_index("section")
    micro_count = segment_input.shape[0]
    row_count = segment_input.shape[2]
    feat_count = segment_input.shape[3]
    width = feat_count * model_count
    head_count = w_query.shape[2] // HEAD
    tract_count = neighbour_ids.shape[2]
    key_span = neighbour_ids.shape[3] * NT
    raw_rows = pool_tokens[:, 0].reshape(-1, pool_tokens.shape[3])
    raw_wide = raw_rows.astype(jnp.float32)
    enc_normed = (raw_wide * rms_scale(raw_wide) * enc_gain).astype(jnp.bfloat16)
    hidden_part = jax.nn.gelu(
        jnp.dot(enc_normed, enc_up, preferred_element_type=jnp.float32)
    ).astype(jnp.bfloat16)
    hidden_full = collect(hidden_part)
    enc_feat = enc_down.shape[1]
    raw_slice = lax.dynamic_slice_in_dim(raw_wide, model_index * enc_feat, enc_feat, 1)
    encoded = (
        raw_slice + jnp.dot(hidden_full, enc_down, preferred_element_type=jnp.float32)
    ).astype(jnp.bfloat16)
    slot_ids = neighbour_ids[:, 0].reshape(-1)
    shard_rows = encoded.shape[0]
    token_index = jnp.arange(NT, dtype=jnp.int32)
    global_rows = ((slot_ids * NT)[:, None] + token_index[None, :]).reshape(-1)
    empty_pool = jnp.zeros((segment_count * shard_rows, enc_feat * model_count), jnp.bfloat16)
    portion = lax.all_gather(encoded, ("section", "mp"), axis=0, tiled=True)
    shard_total = portion.shape[0] // shard_rows

    def one_shard(position, whole_pool):
        shard_block = lax.dynamic_slice_in_dim(portion, position * shard_rows, shard_rows, 0)
        row_start = position // model_count * shard_rows
        col_start = position % model_count * enc_feat
        return lax.dynamic_update_slice(whole_pool, shard_block, (row_start, col_start))

    whole_pool = lax.fori_loop(0, shard_total, one_shard, empty_pool)
    neighbours = jnp.take(whole_pool, global_rows, axis=0)

    def project(weight):
        projected = jnp.dot(neighbours, weight[0], preferred_element_type=jnp.float32).astype(
            jnp.bfloat16
        )
        return projected.reshape(micro_count, tract_count, key_span, head_count, HEAD)

    key_all = project(w_key)
    value_all = project(w_value)
    span_index = jnp.arange(key_span, dtype=jnp.int32) // NT
    usable_all = span_index[None, None, :] < neighbour_counts[:, 0][:, :, None]
    query_cols = w_query[0]
    out_cols = w_out[0]
    query_rows, out_rows = (
        lax.all_to_all(query_cols, "mp", split_axis=0, concat_axis=1, tiled=True),
        lax.all_to_all(out_cols, "mp", split_axis=0, concat_axis=1, tiled=True),
    )
    gain_full = norm_gain[0]
    gain_own = lax.dynamic_slice_in_dim(gain_full, model_index * feat_count, feat_count, 0)
    inputs_own = segment_input[:, 0]
    grads_own = out_grad[:, 0]
    step_count = micro_count + segment_count - 1
    empty_share = jnp.zeros((row_count, feat_count), jnp.bfloat16)
    stored_start = jnp.zeros((micro_count, row_count, width), jnp.bfloat16)

    def forward_step(step, state):
        received, stored = state
        which = step - segment_index
        active = (which >= 0) & (which < micro_count)
        which = jnp.clip(which, 0, micro_count - 1)
        incoming = jnp.where(segment_index == 0, inputs_own[which], received)
        rows_full = collect(incoming)
        outputs = front(
            rows_full,
            gain_full,
            query_cols,
            key_all[which],
            value_all[which],
            usable_all[which],
            head_count,
        )
        attended = collect(outputs[5].reshape(row_count, -1))
        result = incoming.astype(jnp.float32) + jnp.dot(
            attended, out_cols, preferred_element_type=jnp.float32
        )
        stored = stored.at[which].set(jnp.where(active, rows_full, stored[which]))
        return (pass_on(result.astype(jnp.bfloat16), 1), stored)

    _, stored = lax.fori_loop(0, step_count, forward_step, (empty_share, stored_start))
    grad_start = jnp.zeros((micro_count, tract_count, key_span, head_count, HEAD), jnp.bfloat16)

    def backward_step(step, state):
        received, key_grads, value_grads = state
        which = step - (segment_count - 1 - segment_index)
        active = (which >= 0) & (which < micro_count)
        which = jnp.clip(which, 0, micro_count - 1)
        incoming = jnp.where(segment_index == segment_count - 1, grads_own[which], received)
        rows_full = stored[which]
        rows_own = lax.dynamic_slice_in_dim(rows_full, model_index * feat_count, feat_count, 1)
        key_block = key_all[which]
        value_block = value_all[which]
        inv_rms, query_raw, queries, weights, weights_bf, _ = front(
            rows_full, gain_full, query_cols, key_block, value_block, usable_all[which], head_count
        )
        grad_full = collect(incoming)
        grad_att = jnp.dot(grad_full, out_rows.T, preferred_element_type=jnp.float32).astype(
            jnp.bfloat16
        )
        grad_att = grad_att.reshape(queries.shape)
        grad_keys, grad_values, grad_queries = attend_back(
            queries, key_block, value_block, weights, weights_bf, grad_att
        )
        grad_scaled = (grad_queries * HEAD ** (-0.5)).reshape(row_count, -1).astype(jnp.bfloat16)
        part_total = jnp.sum(
            grad_scaled.astype(jnp.float32) * query_raw, axis=1, keepdims=True
        ).astype(jnp.bfloat16)
        scaled_full, totals = collect_pair(grad_scaled, part_total)
        row_total = jnp.sum(totals.astype(jnp.float32), axis=1, keepdims=True)
        grad_normed = jnp.dot(scaled_full, query_rows.T, preferred_element_type=jnp.float32)
        rows_wide = rows_own.astype(jnp.float32)
        grad_in = (
            incoming.astype(jnp.float32)
            + inv_rms * gain_own * grad_normed
            - rows_wide * inv_rms * inv_rms * row_total / width
        )
        key_grads = key_grads.at[which].set(jnp.where(active, grad_keys, key_grads[which]))
        value_grads = value_grads.at[which].set(jnp.where(active, grad_values, value_grads[which]))
        return (pass_on(grad_in.astype(jnp.bfloat16), -1), key_grads, value_grads)

    _, key_grads, value_grads = lax.fori_loop(
        0, step_count, backward_step, (empty_share, grad_start, grad_start)
    )
    contract = (((0,), (0,)), ((), ()))
    key_sum = lax.dot_general(
        neighbours,
        key_grads.reshape(-1, head_count * HEAD),
        contract,
        preferred_element_type=jnp.float32,
    )
    value_sum = lax.dot_general(
        neighbours,
        value_grads.reshape(-1, head_count * HEAD),
        contract,
        preferred_element_type=jnp.float32,
    )
    key_total, value_total = (
        lax.psum(key_sum.astype(jnp.bfloat16), "dp").astype(jnp.float32),
        lax.psum(value_sum.astype(jnp.bfloat16), "dp").astype(jnp.float32),
    )
    return (key_total.astype(jnp.bfloat16)[None], value_total.astype(jnp.bfloat16)[None])


def solution(mesh):
    placed = (
        P(None, "dp", None, "mp"),
        P(None, "dp", None, "mp"),
        P("section", "dp", None, None),
        P(None, "dp", None, None),
        P(None, "dp", None),
        P(),
        P(None, "mp"),
        P(None, "mp"),
        P("section", None),
        P("section", None, "mp"),
        P("section", None, "mp"),
        P("section", None, "mp"),
        P("section", None, "mp"),
    )
    return jax.shard_map(
        on_device,
        mesh=mesh,
        in_specs=placed,
        out_specs=(P("section", None, "mp"), P("section", None, "mp")),
        check_vma=False,
    )
```

profile of v0, /device:TPU:0, one launch (start us, length us, event | category | flops | bytes accessed | tf_op | source)
XLA Modules:
  0.0 1101.6 jit_solution(5113289207940649873)
XLA Ops:
  12.3 4.0 fusion.112
  16.3 80.0 %all-gather.10.cloned.1.call-done = bf16[1024,4096]{1,0:T(8,128)(2,1)} async-done(((bf16[1024,256]{1,0:T(8,128)(2,1)}), bf16[1024,4096]{1,0:T(8,128)(2,1)}) %all-gather.10.cloned.1.call-update) | async-done | bytes 8388624 | tf_op jit(solution)/shard_map/all_gather | solution.py:22
  96.3 6.7 fusion.104
  103.0 5.1 all-to-all-start
  108.5 17.1 %all-to-all-done = bf16[16,256,128]{2,1,0:T(8,128)(2,1)S(1)} async-done(((bf16[16,256,128]{2,1,0:T(8,128)(2,1)}), bf16[16,256,128]{2,1,0:T(8,128)(2,1)S(1)}, u32[]{:S(2)}, u32[]{:S(2)}) %all-to-all-start) | async-done | bytes 1048608 | tf_op jit(solution)/shard_map/all_to_all | solution.py:142
  125.6 3.8 all-to-all-start.1
  133.1 13.0 %all-to-all-done.1 = bf16[16,128,256]{2,1,0:T(8,128)(2,1)S(1)} async-done(((bf16[16,128,256]{2,1,0:T(8,128)(2,1)}), bf16[16,128,256]{2,1,0:T(8,128)(2,1)S(1)}, u32[]{:S(2)}, u32[]{:S(2)}) %all-to-all-start.1) | async-done | bytes 1048608 | tf_op jit(solution)/shard_map/all_to_all | solution.py:141
  148.1 6.3 all-gather.12.cloned.1.call-done
  156.6 184.6 %while.54 = (s32[]{:T(128)}, bf16[2048,896]{1,0:T(8,128)(2,1)}, bf16[32768,56]{0,1:T(8,128)(2,1)}, s32[]{:T(128)}, s32[]{:T(128)}, /*index=5*/s32[]{:T(128)}, s3...) while((s32[]{:T(128)}, bf16[2048,896]{1,0:T(8,128)(2,1)}, ...), condition=%wide.region_2.3_spmd, body=%wide.region_1.2_spmd.sunk | while | flops 26 | bytes 688530 | solution.py:125
  157.7 4.6 dynamic_update_slice.11
  163.4 5.2 dynamic_update_slice.11
  169.7 5.2 dynamic_update_slice.11
  176.0 5.2 dynamic_update_slice.11
  182.3 5.2 dynamic_update_slice.11
  188.6 5.3 dynamic_update_slice.11
  195.0 5.3 dynamic_update_slice.11
  201.3 5.2 dynamic_update_slice.11
  207.7 5.2 dynamic_update_slice.11
  214.0 5.2 dynamic_update_slice.11
  220.3 5.2 dynamic_update_slice.11
  226.6 5.2 dynamic_update_slice.11
  232.9 5.2 dynamic_update_slice.11
  239.2 5.2 dynamic_update_slice.11
  245.5 4.6 dynamic_update_slice.11
  251.2 4.6 dynamic_update_slice.11
  256.9 3.7 dynamic_update_slice.11
  261.6 4.3 dynamic_update_slice.11
  267.1 4.3 dynamic_update_slice.11
  272.5 4.3 dynamic_update_slice.11
  277.9 4.3 dynamic_update_slice.11
  283.3 4.3 dynamic_update_slice.11
  288.8 4.3 dynamic_update_slice.11
  294.2 4.3 dynamic_update_slice.11
  299.6 4.3 dynamic_update_slice.11
  305.0 4.3 dynamic_update_slice.11
  310.4 4.3 dynamic_update_slice.11
  315.8 4.3 dynamic_update_slice.11
  321.2 4.3 dynamic_update_slice.11
  326.6 4.3 dynamic_update_slice.11
  332.0 4.0 dynamic_update_slice.11
  337.2 4.0 dynamic_update_slice.11
  341.2 22.4 %gather_fusion = bf16[4096,896]{1,0:T(8,128)(2,1)} fusion(bf16[2048,896]{1,0:T(8,128)(2,1)} %get-tuple-element.835, s32[4096]{0:T(1024)S(1)} %broadcast_clamp_fusion), kind=kCustom, calls=%fused_computation | custom fusion | bytes 14696448 | tf_op jit(solution)/shard_map/jit(_take)/gather | solution.py:126
  363.6 5.8 convolution_convert_fusion.4
  373.8 5.7 convolution_convert_fusion.5
  385.3 318.6 %while.55 = (s32[]{:T(128)}, bf16[256,128]{1,0:T(8,128)(2,1)S(1)}, bf16[2,256,2048]{2,1,0:T(8,128)(2,1)}, pred[]{:T(512)}, s32[]{:T(128)}, /*index=5*/bf16[2,256...) while((s32[]{:T(128)}, bf16[256,128]{1,0:T(8,128)(2,1)S(1)}, ...), condition=%wide.region_8.9_spmd, body=%wide.region_3.8_spmd.sunk | while | flops 677446400 | bytes 32006564 | solution.py:175
  386.1 45.0 %all-gather.14.cloned.1.call-done = bf16[256,2048]{1,0:T(8,128)(2,1)} async-done(((bf16[256,128]{1,0:T(8,128)(2,1)}), bf16[256,2048]{1,0:T(8,128)(2,1)}) %all-gather.14.cloned.1.call-update) | async-done | bytes 1048592 | tf_op jit(solution)/shard_map/while/body/eval_jaxpr/all_gather | solution.py:22
  441.1 44.5 %all-gather.16.cloned.1.call-done = bf16[256,4096]{1,0:T(8,128)(2,1)} async-done(((bf16[256,256]{1,0:T(8,128)(2,1)}), bf16[256,4096]{1,0:T(8,128)(2,1)}) %all-gather.16.cloned.1.call-update) | async-done | bytes 2097168 | tf_op jit(solution)/shard_map/while/body/eval_jaxpr/all_gather | solution.py:22
  492.2 45.0 %all-gather.14.cloned.1.call-done = bf16[256,2048]{1,0:T(8,128)(2,1)} async-done(((bf16[256,128]{1,0:T(8,128)(2,1)}), bf16[256,2048]{1,0:T(8,128)(2,1)}) %all-gather.14.cloned.1.call-update) | async-done | bytes 1048592 | tf_op jit(solution)/shard_map/while/body/eval_jaxpr/all_gather | solution.py:22
  547.2 44.5 %all-gather.16.cloned.1.call-done = bf16[256,4096]{1,0:T(8,128)(2,1)} async-done(((bf16[256,256]{1,0:T(8,128)(2,1)}), bf16[256,4096]{1,0:T(8,128)(2,1)}) %all-gather.16.cloned.1.call-update) | async-done | bytes 2097168 | tf_op jit(solution)/shard_map/while/body/eval_jaxpr/all_gather | solution.py:22
  598.3 45.2 %all-gather.14.cloned.1.call-done = bf16[256,2048]{1,0:T(8,128)(2,1)} async-done(((bf16[256,128]{1,0:T(8,128)(2,1)}), bf16[256,2048]{1,0:T(8,128)(2,1)}) %all-gather.14.cloned.1.call-update) | async-done | bytes 1048592 | tf_op jit(solution)/shard_map/while/body/eval_jaxpr/all_gather | solution.py:22
  653.6 44.5 %all-gather.16.cloned.1.call-done = bf16[256,4096]{1,0:T(8,128)(2,1)} async-done(((bf16[256,256]{1,0:T(8,128)(2,1)}), bf16[256,4096]{1,0:T(8,128)(2,1)}) %all-gather.16.cloned.1.call-update) | async-done | bytes 2097168 | tf_op jit(solution)/shard_map/while/body/eval_jaxpr/all_gather | solution.py:22
  708.8 323.1 %while.56 = (s32[]{:T(128)}, bf16[256,128]{1,0:T(8,128)(2,1)S(1)}, bf16[2,4,512,2,128]{4,3,2,1,0:T(2,128)(2,1)}, bf16[2,4,512,2,128]{4,3,2,1,0:T(2,128)(2,1)}, p...) while((s32[]{:T(128)}, bf16[256,128]{1,0:T(8,128)(2,1)S(1)}, ...), condition=%wide.region_17.18_spmd, body=%wide.region_9.17_spmd.sunk | while | flops 1152261888 | bytes 76540544 | solution.py:216
  715.5 39.3 %all-gather.18.cloned.1.call-done = bf16[256,2048]{1,0:T(8,128)(2,1)} async-done(((bf16[256,128]{1,0:T(8,128)(2,1)}), bf16[256,2048]{1,0:T(8,128)(2,1)}) %all-gather.18.cloned.1.call-update) | async-done | bytes 1048592 | tf_op jit(solution)/shard_map/while/body/eval_jaxpr/all_gather | solution.py:22
  776.4 3.8 fusion.198
  782.7 22.8 %all-gather.2 = bf16[16,1,256]{2,1,0:T(2,128)(2,1)S(1)} all-gather(bf16[1,1,256]{2,1,0:T(2,128)(2,1)S(1)} %reshape.462), channel_id=1, replica_groups=mesh['section'=2,'dp'=4,'mp'=16] {'mp'}, dimensions={0}, use_global_device_ids=true | all-gather | bytes 8704 | tf_op jit(solution)/shard_map/while/body/eval_jaxpr/all_gather | solution.py:28
  822.7 40.1 %all-gather.18.cloned.1.call-done = bf16[256,2048]{1,0:T(8,128)(2,1)} async-done(((bf16[256,128]{1,0:T(8,128)(2,1)}), bf16[256,2048]{1,0:T(8,128)(2,1)}) %all-gather.18.cloned.1.call-update) | async-done | bytes 1048592 | tf_op jit(solution)/shard_map/while/body/eval_jaxpr/all_gather | solution.py:22
  884.3 3.8 fusion.198
  890.7 22.8 %all-gather.2 = bf16[16,1,256]{2,1,0:T(2,128)(2,1)S(1)} all-gather(bf16[1,1,256]{2,1,0:T(2,128)(2,1)S(1)} %reshape.462), channel_id=1, replica_groups=mesh['section'=2,'dp'=4,'mp'=16] {'mp'}, dimensions={0}, use_global_device_ids=true | all-gather | bytes 8704 | tf_op jit(solution)/shard_map/while/body/eval_jaxpr/all_gather | solution.py:28
  930.7 40.1 %all-gather.18.cloned.1.call-done = bf16[256,2048]{1,0:T(8,128)(2,1)} async-done(((bf16[256,128]{1,0:T(8,128)(2,1)}), bf16[256,2048]{1,0:T(8,128)(2,1)}) %all-gather.18.cloned.1.call-update) | async-done | bytes 1048592 | tf_op jit(solution)/shard_map/while/body/eval_jaxpr/all_gather | solution.py:22
  992.3 3.8 fusion.198
  998.7 22.8 %all-gather.2 = bf16[16,1,256]{2,1,0:T(2,128)(2,1)S(1)} all-gather(bf16[1,1,256]{2,1,0:T(2,128)(2,1)S(1)} %reshape.462), channel_id=1, replica_groups=mesh['section'=2,'dp'=4,'mp'=16] {'mp'}, dimensions={0}, use_global_device_ids=true | all-gather | bytes 8704 | tf_op jit(solution)/shard_map/while/body/eval_jaxpr/all_gather | solution.py:28
  1031.9 7.4 fusion.101
  1039.3 6.7 fusion.98
  1046.1 45.3 %all-reduce.3.cloned.1.call-done = (bf16[1,896,256]{2,1,0:T(8,128)(2,1)}, bf16[1,896,256]{2,1,0:T(8,128)(2,1)}) async-done(((bf16[1,896,256]{2,1,0:T(8,128)(2,1)}, bf16[1,896,256]{2,1,0:T(8,128)(2,1)}), (bf16[1,896,256]{2,1,0:T(8,128)(2,1)}, bf16[1,896,256]{2,1,0:T(8,128)(2,1)})) %all-reduce.3.cloned.1.call-update) | async-done | bytes 917520 | tf_op jit(solution)/shard_map/psum | solution.py:233
  (338 shorter events, 239.3 us)
Async XLA Ops:
  7.2 356.4 %copy-start = (bf16[1,896,256]{2,1,0:T(8,128)(2,1)S(1)}, bf16[1,896,256]{2,1,0:T(8,128)(2,1)}, u32[]{:S(2)}) copy-start(bf16[1,896,256]{2,1,0:T(8,128)(2,1)} %param.35) | copy-start | bytes 1376260
  7.2 2.1 copy-start.9
  7.2 89.1 %all-gather.10.cloned.1.call-start = ((), (), s32[]{:S(2)}) async-start(), calls=%async_computation.2 | async-start | bytes 8912896 | tf_op jit(solution)/shard_map/all_gather | solution.py:22
  9.3 2.9 copy-start.16
  9.3 2.9 copy-start.19
  12.3 84.0 %copy-start.12 = (bf16[4096,56]{0,1:T(8,128)(2,1)S(1)}, bf16[4096,56]{0,1:T(8,128)(2,1)}, u32[]{:S(2)}) copy-start(bf16[4096,56]{0,1:T(8,128)(2,1)} %param.32) | copy-start | bytes 1376260
  16.3 138.2 %all-gather.12.cloned.1.call-start = ((), (), s32[]{:S(2)}) async-start(), calls=%async_computation.3 | async-start | bytes 3784704 | tf_op jit(solution)/shard_map/all_gather | solution.py:116
  103.0 5.1 copy-start.14
  103.0 5.2 copy-start.18
  103.0 5.3 copy-start.15
  103.0 22.6 %all-to-all-start = ((bf16[16,256,128]{2,1,0:T(8,128)(2,1)}), bf16[16,256,128]{2,1,0:T(8,128)(2,1)S(1)}, u32[]{:S(2)}, u32[]{:S(2)}) async-start(bf16[16,256,128]{2,1,0:T(8,128)(2,1)} %bitcast.38), calls=%async_computation | async-start | bytes 2097152 | tf_op jit(solution)/shard_map/all_to_all | solution.py:142
  125.6 20.5 %all-to-all-start.1 = ((bf16[16,128,256]{2,1,0:T(8,128)(2,1)}), bf16[16,128,256]{2,1,0:T(8,128)(2,1)S(1)}, u32[]{:S(2)}, u32[]{:S(2)}) async-start(bf16[16,128,256]{2,1,0:T(8,128)(2,1)} %bitcast.41), calls=%async_computation.1 | async-start | bytes 2097152 | tf_op jit(solution)/shard_map/all_to_all | solution.py:141
  371.9 1.8 copy-start.17
  383.7 1.6 copy-start.10
  383.7 1.6 copy-start.13
  385.3 45.8 %all-gather.14.cloned.1.call-start = ((), (), s32[]{:S(2)}) async-start(), calls=%async_computation.5 | async-start | bytes 1114112 | tf_op jit(solution)/shard_map/while/body/eval_jaxpr/all_gather | solution.py:22
  386.0 99.5 %all-gather.16.cloned.1.call-start = ((), (), s32[]{:S(2)}) async-start(), calls=%async_computation.6 | async-start | bytes 2228224 | tf_op jit(solution)/shard_map/while/body/eval_jaxpr/all_gather | solution.py:22
  438.2 47.4 %copy-start.8 = (bf16[256,128]{1,0:T(8,128)(2,1)S(1)}, bf16[256,128]{1,0:T(8,128)(2,1)}, u32[]{:S(2)}) copy-start(bf16[256,128]{1,0:T(8,128)(2,1)} %bitcast_select_fusion.6) | copy-start | bytes 196612 | tf_op jit(solution)/shard_map/while
  441.1 48.3 %copy-start.2 = (bf16[256,2048]{1,0:T(8,128)(2,1)S(1)}, bf16[256,2048]{1,0:T(8,128)(2,1)}, u32[]{:S(2)}) copy-start(bf16[256,2048]{1,0:T(8,128)(2,1)} %all-gather.14.cloned.1.call-done) | copy-start | bytes 3145732 | tf_op jit(solution)/shard_map/while
  488.2 3.3 collective-permute-start
  491.5 45.7 %all-gather.14.cloned.1.call-start = ((), (), s32[]{:S(2)}) async-start(), calls=%async_computation.5 | async-start | bytes 1114112 | tf_op jit(solution)/shard_map/while/body/eval_jaxpr/all_gather | solution.py:22
  492.1 99.6 %all-gather.16.cloned.1.call-start = ((), (), s32[]{:S(2)}) async-start(), calls=%async_computation.6 | async-start | bytes 2228224 | tf_op jit(solution)/shard_map/while/body/eval_jaxpr/all_gather | solution.py:22
  544.3 47.4 %copy-start.8 = (bf16[256,128]{1,0:T(8,128)(2,1)S(1)}, bf16[256,128]{1,0:T(8,128)(2,1)}, u32[]{:S(2)}) copy-start(bf16[256,128]{1,0:T(8,128)(2,1)} %bitcast_select_fusion.6) | copy-start | bytes 196612 | tf_op jit(solution)/shard_map/while
  547.2 48.3 %copy-start.2 = (bf16[256,2048]{1,0:T(8,128)(2,1)S(1)}, bf16[256,2048]{1,0:T(8,128)(2,1)}, u32[]{:S(2)}) copy-start(bf16[256,2048]{1,0:T(8,128)(2,1)} %all-gather.14.cloned.1.call-done) | copy-start | bytes 3145732 | tf_op jit(solution)/shard_map/while
  594.2 3.3 collective-permute-start
  597.5 46.0 %all-gather.14.cloned.1.call-start = ((), (), s32[]{:S(2)}) async-start(), calls=%async_computation.5 | async-start | bytes 1114112 | tf_op jit(solution)/shard_map/while/body/eval_jaxpr/all_gather | solution.py:22
  598.3 99.8 %all-gather.16.cloned.1.call-start = ((), (), s32[]{:S(2)}) async-start(), calls=%async_computation.6 | async-start | bytes 2228224 | tf_op jit(solution)/shard_map/while/body/eval_jaxpr/all_gather | solution.py:22
  650.7 47.4 %copy-start.8 = (bf16[256,128]{1,0:T(8,128)(2,1)S(1)}, bf16[256,128]{1,0:T(8,128)(2,1)}, u32[]{:S(2)}) copy-start(bf16[256,128]{1,0:T(8,128)(2,1)} %bitcast_select_fusion.6) | copy-start | bytes 196612 | tf_op jit(solution)/shard_map/while
  653.6 48.3 %copy-start.2 = (bf16[256,2048]{1,0:T(8,128)(2,1)S(1)}, bf16[256,2048]{1,0:T(8,128)(2,1)}, u32[]{:S(2)}) copy-start(bf16[256,2048]{1,0:T(8,128)(2,1)} %all-gather.14.cloned.1.call-done) | copy-start | bytes 3145732 | tf_op jit(solution)/shard_map/while
  700.6 3.3 collective-permute-start
  703.9 4.8 copy-start.11
  704.0 4.8 copy-start.20
  708.8 46.0 %all-gather.18.cloned.1.call-start = ((), (), s32[]{:S(2)}) async-start(), calls=%async_computation.7 | async-start | bytes 1114112 | tf_op jit(solution)/shard_map/while/body/eval_jaxpr/all_gather | solution.py:22
  709.5 98.6 %all-gather.20.cloned.1.call-start = ((), (), s32[]{:S(2)}) async-start(), calls=%async_computation.8 | async-start | bytes 2228224 | tf_op jit(solution)/shard_map/while/body/eval_jaxpr/all_gather | solution.py:27
  758.7 2.0 copy-start.21
  765.5 4.8 copy-start.3
  780.2 27.9 %copy-start.7 = (bf16[256,128]{1,0:T(8,128)(2,1)S(1)}, bf16[256,128]{1,0:T(8,128)(2,1)}, u32[]{:S(2)}) copy-start(bf16[256,128]{1,0:T(8,128)(2,1)} %bitcast_select_fusion.7) | copy-start | bytes 196612 | tf_op jit(solution)/shard_map/while
  808.1 4.0 copy-start.4
  810.8 3.8 collective-permute-start.1
  814.6 1.3 copy-start.5
  815.9 46.8 %all-gather.18.cloned.1.call-start = ((), (), s32[]{:S(2)}) async-start(), calls=%async_computation.7 | async-start | bytes 1114112 | tf_op jit(solution)/shard_map/while/body/eval_jaxpr/all_gather | solution.py:22
  816.7 99.4 %all-gather.20.cloned.1.call-start = ((), (), s32[]{:S(2)}) async-start(), calls=%async_computation.8 | async-start | bytes 2228224 | tf_op jit(solution)/shard_map/while/body/eval_jaxpr/all_gather | solution.py:27
  866.6 2.0 copy-start.21
  873.5 4.8 copy-start.3
  888.1 27.9 %copy-start.7 = (bf16[256,128]{1,0:T(8,128)(2,1)S(1)}, bf16[256,128]{1,0:T(8,128)(2,1)}, u32[]{:S(2)}) copy-start(bf16[256,128]{1,0:T(8,128)(2,1)} %bitcast_select_fusion.7) | copy-start | bytes 196612 | tf_op jit(solution)/shard_map/while
  916.1 4.0 copy-start.4
  918.8 3.8 collective-permute-start.1
  922.6 1.3 copy-start.5
  923.9 46.8 %all-gather.18.cloned.1.call-start = ((), (), s32[]{:S(2)}) async-start(), calls=%async_computation.7 | async-start | bytes 1114112 | tf_op jit(solution)/shard_map/while/body/eval_jaxpr/all_gather | solution.py:22
  924.6 99.4 %all-gather.20.cloned.1.call-start = ((), (), s32[]{:S(2)}) async-start(), calls=%async_computation.8 | async-start | bytes 2228224 | tf_op jit(solution)/shard_map/while/body/eval_jaxpr/all_gather | solution.py:27
  974.6 2.0 copy-start.21
  981.5 4.8 copy-start.3
  996.1 27.9 %copy-start.7 = (bf16[256,128]{1,0:T(8,128)(2,1)S(1)}, bf16[256,128]{1,0:T(8,128)(2,1)}, u32[]{:S(2)}) copy-start(bf16[256,128]{1,0:T(8,128)(2,1)} %bitcast_select_fusion.7) | copy-start | bytes 196612 | tf_op jit(solution)/shard_map/while
  1024.0 4.0 copy-start.4
  1026.8 3.8 collective-permute-start.1
  1030.6 1.3 copy-start.5
  1031.9 59.5 %all-reduce.3.cloned.1.call-start = ((), (), s32[]{:S(2)}) async-start(), calls=%async_computation.4 | async-start | bytes 1835008 | tf_op jit(solution)/shard_map/psum | solution.py:233
  1031.9 7.4 copy-start.6
  1039.3 55.7 %copy-start.1 = (bf16[1,896,256]{2,1,0:T(8,128)(2,1)S(1)}, bf16[1,896,256]{2,1,0:T(8,128)(2,1)}, u32[]{:S(2)}) copy-start(bf16[1,896,256]{2,1,0:T(8,128)(2,1)} %param.35) | copy-start | bytes 1376260
Sparse Core Ops, SparseCore 0:
  16.4 79.8 all-gather.9
  103.2 51.2 all-gather.11
  388.8 42.2 all-gather.13
  439.2 46.3 all-gather.15
  494.6 42.4 all-gather.13
  545.2 46.3 all-gather.15
  601.0 42.5 all-gather.13
  651.6 46.3 all-gather.15
  712.3 42.5 all-gather.17
  761.7 46.3 all-gather.19
  819.4 43.2 all-gather.17
  869.6 46.3 all-gather.19
  927.4 43.3 all-gather.17
  977.6 46.3 all-gather.19
  1046.2 45.1 all-reduce.2
where the time goes:
time: 1110 us; the launch traced here: 1100 us
  waiting for transfers between devices  558 us (50%)
  local copies, waits for them, and re-layouts  296 us (27%)
  matrix products  120 us (11%)
  blocking collectives  68.5 us (6%)
  other arithmetic  26 us (2%)
  starting transfers between devices  17 us (2%)
  between operations  13.9 us (1%)
    all_gather x10, waiting for transfers between devices, collect(): return lax.all_gather(tensor, 'mp', axis=1, tiled=True)  468 us
    dynamic_update_slice x32, local copies, waits for them, and re-layouts, one_shard(): lax.dynamic_update_slice(whole_pool, shard_block, (row_start, col_start))  149 us
    all_gather x3, blocking collectives, collect_pair(): lax.all_gather(second, 'mp', axis=1, tiled=True)  68.5 us
    psum x1, waiting for transfers between devices, on_device(): lax.psum(key_sum.astype(jnp.bfloat16), 'dp').astype(jnp.float32)  45.3 us
    dynamic_slice x64, local copies, waits for them, and re-layouts, one_shard(): lax.dynamic_slice_in_dim(portion, position * shard_rows, shard_rows, 0)  34.4 us
    gather x1, local copies, waits for them, and re-layouts, on_device(): neighbours = jnp.take(whole_pool, global_rows, axis=0)  22.4 us
  transfers between devices with their start and end apart: 23, of which 17 were waited for; matrix products, arithmetic and copies ran while one was open for 10% of the time, Pallas kernels for 0%

commit v1 on v0

--- a/solution.py
+++ b/solution.py
@@ -8,6 +8,33 @@
 EPSILON = 1e-05
 
 
+def _follow_series(frame, axis_k):
+    frame = jnp.moveaxis(frame, 0, axis_k)
+    arr_out = frame.shape
+    return frame.reshape(
+        *arr_out[:axis_k], arr_out[axis_k] * arr_out[axis_k + 1], *arr_out[axis_k + 2 :]
+    )
+
+
+def _enter_sheet(u_in, link_axis, pos_dim=1):
+    p_count = lax.axis_size(link_axis)
+    cards = tuple(((dev_j, (dev_j + 1) % p_count) for dev_j in range(p_count)))
+    items = tuple(((ix, dev_i) for dev_i, ix in cards))
+    ready, row_out = ([], [])
+    for d in [*range(p_count - 1)]:
+        if d % 2 == 0:
+            ready.append(
+                lax.ppermute(ready[-1] if ready else u_in, axis_name=link_axis, perm=cards)
+            )
+        else:
+            row_out.append(lax.ppermute(row_out[-1] if row_out else u_in, link_axis, items))
+    opened = jnp.stack([*ready[::-1], u_in, *row_out])
+    response = lax.axis_index(link_axis)
+    clean = response - len(ready)
+    opened = opened[(jnp.arange(p_count) - clean) % p_count]
+    return _follow_series(opened, pos_dim)
+
+
 def passed_along(value, axis, by):
     peers = lax.axis_size(axis)
     pairs = [(i, i + by) for i in range(peers) if 0 <= i + by < peers]
@@ -19,7 +46,7 @@
 
 
 def collect(tensor):
-    return lax.all_gather(tensor, "mp", axis=1, tiled=True)
+    return _enter_sheet(tensor, "mp")
 
 
 def collect_pair(first, second):

time: 1110 us -> 1440 us (1.30)
  starting transfers between devices: 17 us -> 402 us
  waiting for transfers between devices: 558 us -> 361 us
  local copies, waits for them, and re-layouts: 296 us -> 429 us
    all_gather x10 -> x0, waiting for transfers between devices: 468 us -> none  [collect(): return lax.all_gather(tensor, 'mp', axis=1, tiled=True)]
    ppermute x0 -> x150, starting transfers between devices: none -> 386 us  [the longest x70 380 us: _enter_sheet(): lax.ppermute(row_out[-1] if row_out else u_in, link_axis, items)]
    ppermute x0 -> x150, waiting for transfers between devices: none -> 272 us  [the longest x80 248 us: _enter_sheet(): lax.ppermute(ready[-1] if ready else u_in, axis_name=link_axis, perm=cards)]
    while x51 -> x204, local copies, waits for them, and re-layouts: 8.08 us -> 50.6 us
    transpose x0 -> x10, local copies, waits for them, and re-layouts: none -> 25.3 us  [_follow_series(): frame = jnp.moveaxis(frame, 0, axis_k)]
    gather x0 -> x10, local copies, waits for them, and re-layouts: none -> 19.5 us  [_enter_sheet(): opened = opened[(jnp.arange(p_count) - clean) % p_count]]
    unnamed x32 -> x73, local copies, waits for them, and re-layouts: 3.71 us -> 21.4 us
  transfers between devices with their start and end apart: 23 -> 163, of which waited for: 17 -> 82; matrix products, arithmetic and copies ran while one was open for 10% -> 13% of each run, Pallas kernels for 0% -> 0%
where the time goes in v1:
time: 1440 us; the launch traced here: 1430 us
  local copies, waits for them, and re-layouts  429 us (30%)
  starting transfers between devices  402 us (28%)
  waiting for transfers between devices  361 us (25%)
  matrix products  117 us (8%)
  blocking collectives  70.2 us (5%)
  other arithmetic  31.8 us (2%)
    ppermute x70, starting transfers between devices, _enter_sheet(): lax.ppermute(row_out[-1] if row_out else u_in, link_axis, items)  380 us
    ppermute x80, waiting for transfers between devices, _enter_sheet(): lax.ppermute(ready[-1] if ready else u_in, axis_name=link_axis, perm=cards)  248 us
    dynamic_update_slice x32, local copies, waits for them, and re-layouts, one_shard(): lax.dynamic_update_slice(whole_pool, shard_block, (row_start, col_start))  149 us
    all_gather x3, blocking collectives, collect_pair(): lax.all_gather(second, 'mp', axis=1, tiled=True)  70.2 us
    while x204, local copies, waits for them, and re-layouts  50.6 us
    psum x1, waiting for transfers between devices, on_device(): lax.psum(key_sum.astype(jnp.bfloat16), 'dp').astype(jnp.float32)  45.4 us
    dynamic_slice x64, local copies, waits for them, and re-layouts, one_shard(): lax.dynamic_slice_in_dim(portion, position * shard_rows, shard_rows, 0)  34.4 us
  transfers between devices with their start and end apart: 163, of which 82 were waited for; matrix products, arithmetic and copies ran while one was open for 13% of the time, Pallas kernels for 0%

profile of v1, /device:TPU:0, one launch (start us, length us, event | category | flops | bytes accessed | tf_op | source)
XLA Modules:
  0.0 1428.6 jit_solution(11080687093535621749)
XLA Ops:
  17.2 16.8 %collective-permute-done.47 = bf16[1024,256]{1,0:T(8,128)(2,1)S(1)} collective-permute-done((bf16[1024,256]{1,0:T(8,128)(2,1)S(1)}, bf16[1024,256]{1,0:T(8,128)(2,1)S(1)}, u32[]{:S(2)}, u32[]{:S(2)}) %collective-permute-start.47) | collective-permute-done | bytes 524320 | tf_op jit(solution)/shard_map/ppermute | solution.py:27
  39.3 11.1 collective-permute-done.48
  55.7 10.2 collective-permute-done.49
  71.3 9.3 collective-permute-done.50
  80.7 5.4 collective-permute-start.58
  86.1 8.4 collective-permute-done.51
  100.6 6.8 collective-permute-done.52
  107.5 5.9 collective-permute-start.60
  113.5 6.6 collective-permute-done.53
  120.7 5.8 collective-permute-start.61
  126.5 6.4 collective-permute-done.54
  150.7 8.2 gather_fusion.3
  158.9 12.3 copy.94
  171.2 5.6 fusion.103
  181.1 14.1 all-to-all-done
  202.7 9.8 all-to-all-done.1
  214.5 8.1 all-gather.6.cloned.1.call-done
  224.6 184.7 %while.55 = (s32[]{:T(128)}, bf16[2048,896]{1,0:T(8,128)(2,1)}, bf16[32768,56]{0,1:T(8,128)(2,1)}, s32[]{:T(128)}, s32[]{:T(128)}, /*index=5*/s32[]{:T(128)}, s3...) while((s32[]{:T(128)}, bf16[2048,896]{1,0:T(8,128)(2,1)}, ...), condition=%wide.region_2.3_spmd, body=%wide.region_1.2_spmd.sunk | while | flops 26 | bytes 688522 | solution.py:152
  409.4 22.5 %gather_fusion.4 = bf16[4096,896]{1,0:T(8,128)(2,1)} fusion(bf16[2048,896]{1,0:T(8,128)(2,1)} %get-tuple-element.883, s32[4096]{0:T(1024)S(1)} %broadcast_clamp_fusion), kind=kCustom, calls=%fused_computation.4 | custom fusion | bytes 14696448 | tf_op jit(solution)/shard_map/jit(_take)/gather | solution.py:153
  431.8 5.7 convolution_convert_fusion.4
  441.9 5.7 convolution_convert_fusion.5
  453.5 516.1 %while.56 = (s32[]{:T(128)}, bf16[256,128]{1,0:T(8,128)(2,1)S(1)}, bf16[2,256,2048]{2,1,0:T(8,128)(2,1)}, pred[]{:T(512)}, s32[]{:T(128)}, /*index=5*/bf16[2,256...) while((s32[]{:T(128)}, bf16[256,128]{1,0:T(8,128)(2,1)S(1)}, ...), condition=%wide.region_8.9_spmd, body=%wide.region_3.8_spmd.sunk | while | flops 677447680 | bytes 70481320 | solution.py:202
  456.3 6.1 collective-permute-done
  492.8 5.4 collective-permute-start.12
  501.1 5.4 collective-permute-start.13
  508.6 5.4 collective-permute-start.14
  529.4 8.3 collective-permute-done.15
  562.8 5.6 collective-permute-start.26
  626.7 7.6 collective-permute-done
  664.6 5.4 collective-permute-start.12
  672.8 5.4 collective-permute-start.13
  680.4 5.4 collective-permute-start.14
  701.2 8.3 collective-permute-done.15
  734.6 5.6 collective-permute-start.26
  798.5 7.6 collective-permute-done
  836.5 5.4 collective-permute-start.12
  844.6 5.4 collective-permute-start.13
  852.2 5.4 collective-permute-start.14
  873.0 8.3 collective-permute-done.15
  906.4 5.6 collective-permute-start.26
  974.5 387.0 %while.57 = (s32[]{:T(128)}, bf16[256,128]{1,0:T(8,128)(2,1)S(1)}, bf16[2,4,512,2,128]{4,3,2,1,0:T(2,128)(2,1)}, bf16[2,4,512,2,128]{4,3,2,1,0:T(2,128)(2,1)}, p...) while((s32[]{:T(128)}, bf16[256,128]{1,0:T(8,128)(2,1)S(1)}, ...), condition=%wide.region_17.18_spmd, body=%wide.region_9.17_spmd.sunk | while | flops 1152263168 | bytes 91553216 | solution.py:243
  974.7 7.6 collective-permute-done.31
  989.9 5.3 collective-permute-start.40
  1000.0 5.4 collective-permute-start.41
  1007.3 5.7 collective-permute-start.42
  1023.5 5.8 collective-permute-start.44
  1031.2 5.7 collective-permute-start.45
  1067.8 23.4 %all-gather.2 = bf16[16,1,256]{2,1,0:T(2,128)(2,1)S(1)} all-gather(bf16[1,1,256]{2,1,0:T(2,128)(2,1)S(1)} %reshape.700), channel_id=1, replica_groups=mesh['section'=2,'dp'=4,'mp'=16] {'mp'}, dimensions={0}, use_global_device_ids=true | all-gather | bytes 8704 | tf_op jit(solution)/shard_map/while/body/eval_jaxpr/all_gather | solution.py:55
  1104.4 7.0 collective-permute-done.31
  1118.9 5.3 collective-permute-start.40
  1129.0 5.4 collective-permute-start.41
  1136.4 5.7 collective-permute-start.42
  1152.2 5.7 collective-permute-start.44
  1160.2 5.8 collective-permute-start.45
  1196.9 23.4 %all-gather.2 = bf16[16,1,256]{2,1,0:T(2,128)(2,1)S(1)} all-gather(bf16[1,1,256]{2,1,0:T(2,128)(2,1)S(1)} %reshape.700), channel_id=1, replica_groups=mesh['section'=2,'dp'=4,'mp'=16] {'mp'}, dimensions={0}, use_global_device_ids=true | all-gather | bytes 8704 | tf_op jit(solution)/shard_map/while/body/eval_jaxpr/all_gather | solution.py:55
  1233.5 7.0 collective-permute-done.31
  1248.0 5.3 collective-permute-start.40
  1258.2 5.4 collective-permute-start.41
  1265.5 5.7 collective-permute-start.42
  1281.3 5.7 collective-permute-start.44
  1289.3 5.8 collective-permute-start.45
  1326.0 23.4 %all-gather.2 = bf16[16,1,256]{2,1,0:T(2,128)(2,1)S(1)} all-gather(bf16[1,1,256]{2,1,0:T(2,128)(2,1)S(1)} %reshape.700), channel_id=1, replica_groups=mesh['section'=2,'dp'=4,'mp'=16] {'mp'}, dimensions={0}, use_global_device_ids=true | all-gather | bytes 8704 | tf_op jit(solution)/shard_map/while/body/eval_jaxpr/all_gather | solution.py:55
  1361.6 7.4 fusion.97
  1372.8 45.4 %all-reduce.3.cloned.1.call-done = (bf16[1,896,256]{2,1,0:T(8,128)(2,1)}, bf16[1,896,256]{2,1,0:T(8,128)(2,1)}) async-done(((bf16[1,896,256]{2,1,0:T(8,128)(2,1)}, bf16[1,896,256]{2,1,0:T(8,128)(2,1)}), (bf16[1,896,256]{2,1,0:T(8,128)(2,1)}, bf16[1,896,256]{2,1,0:T(8,128)(2,1)})) %all-reduce.3.cloned.1.call-update) | async-done | bytes 917520 | tf_op jit(solution)/shard_map/psum | solution.py:260
  (867 shorter events, 886.0 us)
Async XLA Ops:
  7.2 215.4 %all-gather.6.cloned.1.call-start = ((), (), s32[]{:S(2)}) async-start(), calls=%async_computation.2 | async-start | bytes 3784704 | tf_op jit(solution)/shard_map/all_gather | solution.py:143
  15.4 18.6 %collective-permute-start.47 = (bf16[1024,256]{1,0:T(8,128)(2,1)S(1)}, bf16[1024,256]{1,0:T(8,128)(2,1)S(1)}, u32[]{:S(2)}, u32[]{:S(2)}) collective-permute-start(bf16[1024,256]{1,0:T(8,128)(2,1)S(1)} %fusion.111), channel_id=1, source_target_pairs={{0,1},{1,2},{2,3},{3,4},{4,5},{5,6},{6,7},{7,8},{8,9},{9,10},{10,1... | collective-permute-start | bytes 1572872 | tf_op jit(solution)/shard_map/ppermute | solution.py:27
  34.0 16.4 %collective-permute-start.48 = (bf16[1024,256]{1,0:T(8,128)(2,1)S(1)}, bf16[1024,256]{1,0:T(8,128)(2,1)S(1)}, u32[]{:S(2)}, u32[]{:S(2)}) collective-permute-start(bf16[1024,256]{1,0:T(8,128)(2,1)S(1)} %collective-permute-done.47), channel_id=1, source_target_pairs={{0,1},{1,2},{2,3},{3,4},{4,5},{5,6},{6,7},{7,8},{8,9},{9,10},{10,1... | collective-permute-start | bytes 1572872 | tf_op jit(solution)/shard_map/ppermute | solution.py:27
  34.0 16.4 %collective-permute-start.55 = (bf16[1024,256]{1,0:T(8,128)(2,1)S(1)}, bf16[1024,256]{1,0:T(8,128)(2,1)S(1)}, u32[]{:S(2)}, u32[]{:S(2)}) collective-permute-start(bf16[1024,256]{1,0:T(8,128)(2,1)S(1)} %fusion.111), channel_id=1, source_target_pairs={{1,0},{2,1},{3,2},{4,3},{5,4},{6,5},{7,6},{8,7},{9,8},{10,9},{11,1... | collective-permute-start | bytes 1572872 | tf_op jit(solution)/shard_map/ppermute | solution.py:30
  50.4 15.6 %collective-permute-start.49 = (bf16[1024,256]{1,0:T(8,128)(2,1)S(1)}, bf16[1024,256]{1,0:T(8,128)(2,1)S(1)}, u32[]{:S(2)}, u32[]{:S(2)}) collective-permute-start(bf16[1024,256]{1,0:T(8,128)(2,1)S(1)} %collective-permute-done.48), channel_id=1, source_target_pairs={{0,1},{1,2},{2,3},{3,4},{4,5},{5,6},{6,7},{7,8},{8,9},{9,10},{10,1... | collective-permute-start | bytes 1572872 | tf_op jit(solution)/shard_map/ppermute | solution.py:27
  50.4 15.6 %collective-permute-start.56 = (bf16[1024,256]{1,0:T(8,128)(2,1)S(1)}, bf16[1024,256]{1,0:T(8,128)(2,1)S(1)}, u32[]{:S(2)}, u32[]{:S(2)}) collective-permute-start(bf16[1024,256]{1,0:T(8,128)(2,1)S(1)} %collective-permute-done.55), channel_id=1, source_target_pairs={{1,0},{2,1},{3,2},{4,3},{5,4},{6,5},{7,6},{8,7},{9,8},{10,9},{11,1... | collective-permute-start | bytes 1572872 | tf_op jit(solution)/shard_map/ppermute | solution.py:30
  66.0 14.7 %collective-permute-start.50 = (bf16[1024,256]{1,0:T(8,128)(2,1)S(1)}, bf16[1024,256]{1,0:T(8,128)(2,1)S(1)}, u32[]{:S(2)}, u32[]{:S(2)}) collective-permute-start(bf16[1024,256]{1,0:T(8,128)(2,1)S(1)} %collective-permute-done.49), channel_id=1, source_target_pairs={{0,1},{1,2},{2,3},{3,4},{4,5},{5,6},{6,7},{7,8},{8,9},{9,10},{10,1... | collective-permute-start | bytes 1572872 | tf_op jit(solution)/shard_map/ppermute | solution.py:27
  66.0 14.7 %collective-permute-start.57 = (bf16[1024,256]{1,0:T(8,128)(2,1)S(1)}, bf16[1024,256]{1,0:T(8,128)(2,1)S(1)}, u32[]{:S(2)}, u32[]{:S(2)}) collective-permute-start(bf16[1024,256]{1,0:T(8,128)(2,1)S(1)} %collective-permute-done.56), channel_id=1, source_target_pairs={{1,0},{2,1},{3,2},{4,3},{5,4},{6,5},{7,6},{8,7},{9,8},{10,9},{11,1... | collective-permute-start | bytes 1572872 | tf_op jit(solution)/shard_map/ppermute | solution.py:30
  80.7 13.8 collective-permute-start.51
  80.7 13.8 collective-permute-start.58
  94.5 13.0 collective-permute-start.52
  95.3 12.2 collective-permute-start.59
  107.5 12.6 collective-permute-start.53
  107.5 13.1 collective-permute-start.60
  120.1 12.8 collective-permute-start.54
  120.7 29.1 %collective-permute-start.61 = (bf16[1024,256]{1,0:T(8,128)(2,1)}, bf16[1024,256]{1,0:T(8,128)(2,1)S(1)}, u32[]{:S(2)}, u32[]{:S(2)}) collective-permute-start(bf16[1024,256]{1,0:T(8,128)(2,1)} %collective-permute-done.60), channel_id=1, source_target_pairs={{1,0},{2,1},{3,2},{4,3},{5,4},{6,5},{7,6},{8,7},{9,8},{10,9},{11,1... | collective-permute-start | bytes 1572872 | tf_op jit(solution)/shard_map/ppermute | solution.py:30
  176.9 18.3 %all-to-all-start = ((bf16[16,256,128]{2,1,0:T(8,128)(2,1)}), bf16[16,256,128]{2,1,0:T(8,128)(2,1)S(1)}, u32[]{:S(2)}, u32[]{:S(2)}) async-start(bf16[16,256,128]{2,1,0:T(8,128)(2,1)} %bitcast.111), calls=%async_computation | async-start | bytes 2097152 | tf_op jit(solution)/shard_map/all_to_all | solution.py:169
  195.2 17.3 %all-to-all-start.1 = ((bf16[16,128,256]{2,1,0:T(8,128)(2,1)}), bf16[16,128,256]{2,1,0:T(8,128)(2,1)S(1)}, u32[]{:S(2)}, u32[]{:S(2)}) async-start(bf16[16,128,256]{2,1,0:T(8,128)(2,1)} %bitcast.114), calls=%async_computation.1 | async-start | bytes 2097152 | tf_op jit(solution)/shard_map/all_to_all | solution.py:168
  529.4 8.4 collective-permute-start.15
  537.7 8.3 collective-permute-start.23
  554.3 8.5 collective-permute-start.18
  554.3 8.5 collective-permute-start.25
  562.8 9.3 collective-permute-start.19
  562.8 9.3 collective-permute-start.26
  572.1 8.4 collective-permute-start.20
  572.1 14.4 %collective-permute-start.27 = (bf16[256,256]{1,0:T(8,128)(2,1)S(1)}, bf16[256,256]{1,0:T(8,128)(2,1)}, u32[]{:S(2)}, u32[]{:S(2)}) collective-permute-start(bf16[256,256]{1,0:T(8,128)(2,1)S(1)} %collective-permute-done.26), channel_id=1, source_target_pairs={{1,0},{2,1},{3,2},{4,3},{5,4},{6,5},{7,6},{8,7},{9,8},{10,9},{11,1... | collective-permute-start | bytes 393224 | tf_op jit(solution)/shard_map/while/body/eval_jaxpr/ppermute | solution.py:30
  580.5 11.4 collective-permute-start.21
  586.5 8.9 collective-permute-start.28
  591.9 8.9 collective-permute-start.22
  595.5 19.8 %collective-permute-start.29 = (bf16[256,256]{1,0:T(8,128)(2,1)}, bf16[256,256]{1,0:T(8,128)(2,1)S(1)}, u32[]{:S(2)}, u32[]{:S(2)}) collective-permute-start(bf16[256,256]{1,0:T(8,128)(2,1)} %collective-permute-done.28), channel_id=1, source_target_pairs={{1,0},{2,1},{3,2},{4,3},{5,4},{6,5},{7,6},{8,7},{9,8},{10,9},{11,1... | collective-permute-start | bytes 393224 | tf_op jit(solution)/shard_map/while/body/eval_jaxpr/ppermute | solution.py:30
  701.1 8.4 collective-permute-start.15
  709.4 8.3 collective-permute-start.23
  726.0 8.6 collective-permute-start.18
  726.0 8.6 collective-permute-start.25
  734.6 9.4 collective-permute-start.19
  734.6 9.4 collective-permute-start.26
  744.0 8.4 collective-permute-start.20
  744.0 14.4 %collective-permute-start.27 = (bf16[256,256]{1,0:T(8,128)(2,1)S(1)}, bf16[256,256]{1,0:T(8,128)(2,1)}, u32[]{:S(2)}, u32[]{:S(2)}) collective-permute-start(bf16[256,256]{1,0:T(8,128)(2,1)S(1)} %collective-permute-done.26), channel_id=1, source_target_pairs={{1,0},{2,1},{3,2},{4,3},{5,4},{6,5},{7,6},{8,7},{9,8},{10,9},{11,1... | collective-permute-start | bytes 393224 | tf_op jit(solution)/shard_map/while/body/eval_jaxpr/ppermute | solution.py:30
  752.4 11.4 collective-permute-start.21
  758.4 8.9 collective-permute-start.28
  763.7 8.9 collective-permute-start.22
  767.3 19.8 %collective-permute-start.29 = (bf16[256,256]{1,0:T(8,128)(2,1)}, bf16[256,256]{1,0:T(8,128)(2,1)S(1)}, u32[]{:S(2)}, u32[]{:S(2)}) collective-permute-start(bf16[256,256]{1,0:T(8,128)(2,1)} %collective-permute-done.28), channel_id=1, source_target_pairs={{1,0},{2,1},{3,2},{4,3},{5,4},{6,5},{7,6},{8,7},{9,8},{10,9},{11,1... | collective-permute-start | bytes 393224 | tf_op jit(solution)/shard_map/while/body/eval_jaxpr/ppermute | solution.py:30
  872.9 8.4 collective-permute-start.15
  881.3 8.3 collective-permute-start.23
  897.9 8.6 collective-permute-start.18
  897.9 8.6 collective-permute-start.25
  906.4 9.4 collective-permute-start.19
  906.4 9.4 collective-permute-start.26
  915.9 8.4 collective-permute-start.20
  915.9 14.4 %collective-permute-start.27 = (bf16[256,256]{1,0:T(8,128)(2,1)S(1)}, bf16[256,256]{1,0:T(8,128)(2,1)}, u32[]{:S(2)}, u32[]{:S(2)}) collective-permute-start(bf16[256,256]{1,0:T(8,128)(2,1)S(1)} %collective-permute-done.26), channel_id=1, source_target_pairs={{1,0},{2,1},{3,2},{4,3},{5,4},{6,5},{7,6},{8,7},{9,8},{10,9},{11,1... | collective-permute-start | bytes 393224 | tf_op jit(solution)/shard_map/while/body/eval_jaxpr/ppermute | solution.py:30
  924.2 11.4 collective-permute-start.21
  930.3 8.9 collective-permute-start.28
  935.6 8.9 collective-permute-start.22
  939.2 19.8 %collective-permute-start.29 = (bf16[256,256]{1,0:T(8,128)(2,1)}, bf16[256,256]{1,0:T(8,128)(2,1)S(1)}, u32[]{:S(2)}, u32[]{:S(2)}) collective-permute-start(bf16[256,256]{1,0:T(8,128)(2,1)} %collective-permute-done.28), channel_id=1, source_target_pairs={{1,0},{2,1},{3,2},{4,3},{5,4},{6,5},{7,6},{8,7},{9,8},{10,9},{11,1... | collective-permute-start | bytes 393224 | tf_op jit(solution)/shard_map/while/body/eval_jaxpr/ppermute | solution.py:30
  974.5 120.7 %all-gather.8.cloned.1.call-start = ((), (), s32[]{:S(2)}) async-start(), calls=%async_computation.4 | async-start | bytes 2228224 | tf_op jit(solution)/shard_map/while/body/eval_jaxpr/all_gather | solution.py:54
  989.9 10.1 collective-permute-start.40
  1007.3 8.5 collective-permute-start.42
  1103.1 121.3 %all-gather.8.cloned.1.call-start = ((), (), s32[]{:S(2)}) async-start(), calls=%async_computation.4 | async-start | bytes 2228224 | tf_op jit(solution)/shard_map/while/body/eval_jaxpr/all_gather | solution.py:54
  1118.9 10.1 collective-permute-start.40
  1136.4 8.5 collective-permute-start.42
  1232.2 121.3 %all-gather.8.cloned.1.call-start = ((), (), s32[]{:S(2)}) async-start(), calls=%async_computation.4 | async-start | bytes 2228224 | tf_op jit(solution)/shard_map/while/body/eval_jaxpr/all_gather | solution.py:54
  1248.0 10.1 collective-permute-start.40
  1265.5 8.5 collective-permute-start.42
  1361.5 56.7 %all-reduce.3.cloned.1.call-start = ((), (), s32[]{:S(2)}) async-start(), calls=%async_computation.3 | async-start | bytes 1835008 | tf_op jit(solution)/shard_map/psum | solution.py:260
  (157 other events, 2220.1 us)
Sparse Core Ops, SparseCore 0:
  177.0 45.4 all-gather.5
  1046.7 48.5 all-gather.7
  1175.8 48.5 all-gather.7
  1304.9 48.5 all-gather.7
  1372.9 45.1 all-reduce.2
